TPU v7x, 32 devices: a whole 2x2x4 slice. The times are simulated.
32 devices in a mesh: groups: 1, wide: 8 (over y, x, core), narrow: 4 (over z).
Axes of the slice: x: 2, y: 2, z: 4, core: 2. Of those that a mesh axis runs over, the one named last changes fastest.
Arguments:
- table_cells: bfloat16 [128, 128, 192], P(('groups', 'wide', 'narrow')), may hold values from -12 to 12
- counts: int32 [128], P(('groups', 'wide', 'narrow')), may hold values from 32 to 128, as said below
- train_count: int32 [1], P('groups'), may hold values from 32 to 96
- norm_gain: float32 [3, 192], replicated, may hold values from 0.5 to 1.5
- feature_in: bfloat16 [192, 576], P('narrow'), may hold values from -0.4375 to 0.4375
- feature_out: bfloat16 [192, 192], P('narrow'), may hold values from -0.4375 to 0.4375
- sample_in: bfloat16 [192, 576], P('narrow'), may hold values from -0.4375 to 0.4375
- sample_out: bfloat16 [192, 192], P('narrow'), may hold values from -0.4375 to 0.4375
- hidden_up: bfloat16 [192, 768], P('narrow'), may hold values from -0.4375 to 0.4375
- hidden_down: bfloat16 [768, 192], P('narrow'), may hold values from -0.21875 to 0.21875
Outputs:
- updated_cells: bfloat16 [128, 128, 192], P(('groups', 'wide', 'narrow'))
Inputs may be any that keep to these rules, and one draw needn't show every extreme that they name: `counts`: feature j of a row is present when j < its count; some row has all 128 features present. Rows 0 to train_count - 1 are the training rows.
All inputs are finite; a program needn't handle non-finite values.
Results may differ from a plain program's by a relative error of at most 0.0086.
Values may be sent and summed in bfloat16 or wider, within the bound.
A program may use at most 64 MiB of HBM per device.

v0:
```python
import jax
import jax.numpy as jnp
from jax import lax
from jax.sharding import PartitionSpec as P

HEADS = 6
epsilon = 1e-05


def normalize(values, gain):
    average = jnp.mean(values, axis=-1, keepdims=True)
    centered = values - average
    spread = jnp.mean(centered * centered, axis=-1, keepdims=True)
    return centered * lax.rsqrt(spread + epsilon) * gain


def attend(packed, valid, head_count):
    length = packed.shape[0]
    model_width = packed.shape[1] // 3
    head_size = model_width // head_count
    scale_factor = 1.0 / jnp.sqrt(jnp.float32(head_size))
    queries = packed[:, :model_width].reshape(length, head_count, head_size)
    key_part = packed[:, model_width : 2 * model_width].reshape(length, head_count, head_size)
    value_part = packed[:, 2 * model_width :].reshape(length, head_count, head_size)
    scores = (
        jnp.einsum("qhd,khd->hqk", queries, key_part, preferred_element_type=jnp.float32)
        * scale_factor
    )
    scores = jnp.where(valid[None, None, :], scores, jnp.float32(-1e30))
    maxima = jnp.max(scores, axis=-1, keepdims=True)
    exponentials = jnp.where(valid[None, None, :], jnp.exp(scores - maxima), jnp.float32(0.0))
    totals = jnp.sum(exponentials, axis=-1, keepdims=True)
    probabilities = (exponentials / totals).astype(jnp.bfloat16)
    context = jnp.einsum(
        "hqk,khd->qhd", probabilities, value_part, preferred_element_type=jnp.float32
    )
    return context.reshape(length, model_width).astype(jnp.bfloat16)


def project(values, weight):
    flat = values.reshape(-1, values.shape[-1])
    return jnp.dot(flat, weight, preferred_element_type=jnp.float32).reshape(
        values.shape[:-1] + (weight.shape[1],)
    )


def body(
    table_cells,
    counts,
    train_count,
    norm_gain,
    feature_in,
    feature_out,
    sample_in,
    sample_out,
    hidden_up,
    hidden_down,
):
    row_local, feats_all, model_width = table_cells.shape
    feat_in_all, feat_out_all = (
        lax.all_gather(feature_in, "narrow", axis=0, tiled=True),
        lax.all_gather(feature_out, "narrow", axis=0, tiled=True),
    )
    feature_ids = jnp.arange(feats_all, dtype=jnp.int32)
    packed = project(table_cells, feat_in_all).astype(jnp.bfloat16)

    def feature_row(pair):
        return attend(pair[0], feature_ids < pair[1], HEADS)

    context = lax.map(feature_row, (packed, counts))
    update = project(context, feat_out_all)
    first = normalize(table_cells.astype(jnp.float32) + update, norm_gain[0]).astype(jnp.bfloat16)
    columns = lax.all_to_all(first, ("wide", "narrow"), split_axis=1, concat_axis=0, tiled=True)
    rows_all, feat_local = (columns.shape[0], columns.shape[1])
    samp_in_all, samp_out_all = (
        lax.all_gather(sample_in, "narrow", axis=0, tiled=True),
        lax.all_gather(sample_out, "narrow", axis=0, tiled=True),
    )
    by_feature = jnp.swapaxes(columns, 0, 1)
    valid = jnp.arange(rows_all, dtype=jnp.int32) < train_count[0]
    packed_samples = project(by_feature, samp_in_all).astype(jnp.bfloat16)
    sample_context = lax.map(lambda column: attend(column, valid, HEADS), packed_samples)
    sample_update = project(sample_context, samp_out_all)
    second = normalize(by_feature.astype(jnp.float32) + sample_update, norm_gain[1]).astype(
        jnp.bfloat16
    )
    up_all, down_all = (
        lax.all_gather(hidden_up, "narrow", axis=0, tiled=True),
        lax.all_gather(hidden_down, "narrow", axis=0, tiled=True),
    )
    hidden = jax.nn.gelu(project(second, up_all), approximate=False).astype(jnp.bfloat16)
    back = project(hidden, down_all)
    result = normalize(second.astype(jnp.float32) + back, norm_gain[2]).astype(jnp.bfloat16)
    result_rows = jnp.swapaxes(result, 0, 1)
    return lax.all_to_all(result_rows, ("wide", "narrow"), split_axis=0, concat_axis=1, tiled=True)


def solution(mesh):
    return jax.shard_map(
        body,
        mesh=mesh,
        in_specs=(
            P(("groups", "wide", "narrow"), None, None),
            P(("groups", "wide", "narrow")),
            P("groups"),
            P(),
            P("narrow", None),
            P("narrow", None),
            P("narrow", None),
            P("narrow", None),
            P("narrow", None),
            P("narrow", None),
        ),
        out_specs=P(("groups", "wide", "narrow"), None, None),
        check_vma=False,
    )
```

profile of v0, /device:TPU:0, one launch (start us, length us, event | category | flops | bytes accessed | tf_op | source)
XLA Modules:
  0.0 134.4 jit_solution(16577640377260590868)
XLA Ops:
  0.0 0.8 fusion.94
  0.8 15.2 %all_gather.19 = bf16[192,192]{1,0:T(8,128)(2,1)S(1)} all-gather(bf16[48,192]{1,0:T(8,128)(2,1)} %param.19), channel_id=1, replica_groups=mesh['groups'=1,'wide'=8,'narrow'=4] {'narrow'}, dimensions={0}, use_global_device_ids=true | all-gather | bytes 92160 | tf_op jit(solution)/shard_map/all_gather | solution.py:62
  16.0 14.4 %all_gather.18 = bf16[192,576]{1,0:T(8,128)(2,1)S(1)} all-gather(bf16[48,576]{1,0:T(8,128)(2,1)} %param.18), channel_id=1, replica_groups=mesh['groups'=1,'wide'=8,'narrow'=4] {'narrow'}, dimensions={0}, use_global_device_ids=true | all-gather | bytes 276480 | tf_op jit(solution)/shard_map/all_gather | solution.py:61
  30.5 1.3 convolution_convert_fusion.3
  31.8 9.3 %while.22 = (s32[]{:T(128)}, bf16[4,128,192]{1,2,0:T(8,128)(2,1)S(1)}, bf16[4,128,576]{1,2,0:T(8,128)(2,1)S(1)}, s32[4]{0:T(128)S(1)}, s32[]{:T(128)}) while((s32[]{:T(128)}, bf16[4,128,192]{1,2,0:T(8,128)(2,1)S(1)}, bf16[4,128,576]{1,2,0:T(8,128)(2,1)S(1)}, s32[4]{0:T(128)S(1)}, s32[]{:T(128)}) %tuple.61), condition=%wide.region_3.4_spmd.clone, body=%wide.region_0.3_spmd.clone.sunk | while | flops 19981440 | bytes 1776221 | solution.py:70
  31.8 0.7 dynamic_slice.20
  32.5 0.7 iota_compare_fusion.4
  34.1 0.7 dynamic_slice.20
  34.8 0.7 iota_compare_fusion.4
  36.5 0.7 dynamic_slice.20
  37.1 0.7 iota_compare_fusion.4
  38.8 0.7 dynamic_slice.20
  39.5 0.7 iota_compare_fusion.4
  41.6 0.9 copy.28
  42.5 5.3 %all-to-all-start = ((bf16[4,128,192]{2,0,1:T(4,128)(2,1)}), bf16[4,128,192]{2,0,1:T(4,128)(2,1)S(1)}, u32[]{:S(2)}, u32[]{:S(2)}) async-start(bf16[4,128,192]{2,0,1:T(4,128)(2,1)} %copy.28), calls=%async_computation | async-start | bytes 524288 | tf_op jit(solution)/shard_map/all_to_all | solution.py:73
  47.8 16.4 %all_gather.21 = bf16[192,192]{1,0:T(8,128)(2,1)S(1)} all-gather(bf16[48,192]{1,0:T(8,128)(2,1)S(1)} %copy-done.4), channel_id=1, replica_groups=mesh['groups'=1,'wide'=8,'narrow'=4] {'narrow'}, dimensions={0}, use_global_device_ids=true | all-gather | bytes 92160 | tf_op jit(solution)/shard_map/all_gather | solution.py:77
  64.3 13.8 %all_gather.20 = bf16[192,576]{1,0:T(8,128)(2,1)S(1)} all-gather(bf16[48,576]{1,0:T(8,128)(2,1)S(1)} %copy-done.3), channel_id=1, replica_groups=mesh['groups'=1,'wide'=8,'narrow'=4] {'narrow'}, dimensions={0}, use_global_device_ids=true | all-gather | bytes 276480 | tf_op jit(solution)/shard_map/all_gather | solution.py:76
  78.1 14.3 %all_gather.22 = bf16[192,768]{1,0:T(8,128)(2,1)S(1)} all-gather(bf16[48,768]{1,0:T(8,128)(2,1)S(1)} %copy-done.2), channel_id=1, replica_groups=mesh['groups'=1,'wide'=8,'narrow'=4] {'narrow'}, dimensions={0}, use_global_device_ids=true | all-gather | bytes 368640 | tf_op jit(solution)/shard_map/all_gather | solution.py:88
  92.3 14.2 %all_gather.23 = bf16[768,192]{1,0:T(8,128)(2,1)S(1)} all-gather(bf16[192,192]{1,0:T(8,128)(2,1)S(1)} %copy-done.1), channel_id=1, replica_groups=mesh['groups'=1,'wide'=8,'narrow'=4] {'narrow'}, dimensions={0}, use_global_device_ids=true | all-gather | bytes 368640 | tf_op jit(solution)/shard_map/all_gather | solution.py:89
  107.3 6.4 %while.23 = (s32[]{:T(128)}, bf16[4,128,192]{1,2,0:T(8,128)(2,1)S(1)}, bf16[4,128,576]{1,2,0:T(8,128)(2,1)S(1)}, s32[]{:T(128)}, s32[]{:T(128)}) while((s32[]{:T(128)}, bf16[4,128,192]{1,2,0:T(8,128)(2,1)S(1)}, bf16[4,128,576]{1,2,0:T(8,128)(2,1)S(1)}, s32[]{:T(128)}, s32[]{:T(128)}) %tuple.58), condition=%wide.region_9.10_spmd.clone, body=%wide.region_6.9_spmd.clone.sunk | while | flops 19981440 | bytes 1776209 | solution.py:82
  114.2 0.8 fusion.43
  115.0 3.8 %fusion.46 = (f32[4,128]{1,0:T(4,128)S(1)}, f32[4,128,192]{1,2,0:T(8,128)S(1)}) fusion(bf16[4,128,192]{1,2,0:T(8,128)(2,1)S(1)} %multiply_convert_fusion, bf16[768,192]{1,0:T(8,128)(2,1)S(1)} %all_gather.23, f32[4,128,768]{2,1,0:T(8,128)S(1)} %get-tuple-element.114, u8[128,768]{1,0:T(8,128)(4,1)S(1)} %get-tuple-element.78, ...), kind=kOutput, calls=%fused_computation.80 | convolution fusion | flops 178814464 | bytes 2656256 | tf_op jit(solution)/shard_map/dot_general | solution.py:42
  119.2 14.2 %all_to_all.36 = bf16[128,4,192]{2,1,0:T(4,128)(2,1)S(1)} all-to-all(bf16[128,4,192]{2,1,0:T(4,128)(2,1)S(1)} %copy.33), channel_id=1, replica_groups=mesh['groups'=1,'wide'=8,'narrow'=4] {'wide','narrow'}, dimensions={0} | all-to-all | bytes 393216 | tf_op jit(solution)/shard_map/all_to_all | solution.py:95
  133.6 0.9 copy.35
  (86 shorter events, 12.1 us)
Async XLA Ops:
  0.0 31.8 %copy-start.5 = (s32[4]{0:T(128)S(1)}, s32[4]{0:T(128)}, u32[]{:S(2)}) copy-start(s32[4]{0:T(128)} %param.15) | copy-start | bytes 52
  31.8 9.3 %copy-start = (bf16[4,128,192]{1,2,0:T(8,128)(2,1)S(1)}, bf16[4,128,192]{1,2,0:T(8,128)(2,1)}, u32[]{:S(2)}) copy-start(bf16[4,128,192]{1,2,0:T(8,128)(2,1)} %param.14) | copy-start | bytes 589828
  41.1 6.7 %copy-start.4 = (bf16[48,192]{1,0:T(8,128)(2,1)S(1)}, bf16[48,192]{1,0:T(8,128)(2,1)}, u32[]{:S(2)}) copy-start(bf16[48,192]{1,0:T(8,128)(2,1)} %param.21) | copy-start | bytes 55300
  41.1 23.2 %copy-start.3 = (bf16[48,576]{1,0:T(8,128)(2,1)S(1)}, bf16[48,576]{1,0:T(8,128)(2,1)}, u32[]{:S(2)}) copy-start(bf16[48,576]{1,0:T(8,128)(2,1)} %param.20) | copy-start | bytes 165892
  41.1 36.9 %copy-start.2 = (bf16[48,768]{1,0:T(8,128)(2,1)S(1)}, bf16[48,768]{1,0:T(8,128)(2,1)}, u32[]{:S(2)}) copy-start(bf16[48,768]{1,0:T(8,128)(2,1)} %param.22) | copy-start | bytes 221188
  41.4 50.9 %copy-start.1 = (bf16[192,192]{1,0:T(8,128)(2,1)S(1)}, bf16[192,192]{1,0:T(8,128)(2,1)}, u32[]{:S(2)}) copy-start(bf16[192,192]{1,0:T(8,128)(2,1)} %param.23) | copy-start | bytes 221188
  42.5 64.1 %all-to-all-start = ((bf16[4,128,192]{2,0,1:T(4,128)(2,1)}), bf16[4,128,192]{2,0,1:T(4,128)(2,1)S(1)}, u32[]{:S(2)}, u32[]{:S(2)}) async-start(bf16[4,128,192]{2,0,1:T(4,128)(2,1)} %copy.28), calls=%async_computation | async-start | bytes 524288 | tf_op jit(solution)/shard_map/all_to_all | solution.py:73
where the time goes:
time: 135 us; the launch traced here: 134 us
  blocking collectives  103 us (76%)
  matrix products  13.6 us (10%)
  local copies, waits for them, and re-layouts  6.32 us (5%)
  other arithmetic  5.99 us (4%)
  starting transfers between devices  5.33 us (4%)
    all_gather x1, blocking collectives, body(): lax.all_gather(sample_out, 'narrow', axis=0, tiled=True)  16.4 us
    all_gather x1, blocking collectives, body(): lax.all_gather(feature_out, 'narrow', axis=0, tiled=True)  15.2 us
    all_gather x1, blocking collectives, body(): lax.all_gather(feature_in, 'narrow', axis=0, tiled=True)  14.4 us
    all_gather x1, blocking collectives, body(): lax.all_gather(hidden_up, 'narrow', axis=0, tiled=True)  14.3 us
    all_to_all x1, blocking collectives, body(): lax.all_to_all(result_rows, ('wide', 'narrow'), split_axis=0, concat_axis...  14.2 us
    all_gather x1, blocking collectives, body(): lax.all_gather(hidden_down, 'narrow', axis=0, tiled=True)  14.2 us
    all_gather x1, blocking collectives, body(): lax.all_gather(sample_in, 'narrow', axis=0, tiled=True)  13.8 us
    dot_general x6, matrix products, project(): jnp.dot(flat, weight, preferred_element_type=jnp.float32)  6.72 us
  transfers between devices with their start and end apart: 1, of which 0 were waited for; matrix products, arithmetic and copies ran while one was open for 0% of the time, Pallas kernels for 0%

commit v1 on v0

--- a/solution.py
+++ b/solution.py
@@ -92,7 +92,15 @@
     back = project(hidden, down_all)
     result = normalize(second.astype(jnp.float32) + back, norm_gain[2]).astype(jnp.bfloat16)
     result_rows = jnp.swapaxes(result, 0, 1)
-    return lax.all_to_all(result_rows, ("wide", "narrow"), split_axis=0, concat_axis=1, tiled=True)
+    return jnp.concatenate(
+        lax.all_to_all(
+            jnp.stack(jnp.split(result_rows, lax.axis_size(("wide", "narrow")), axis=0)),
+            ("wide", "narrow"),
+            0,
+            0,
+        ),
+        axis=1,
+    )
 
 
 def solution(mesh):

time: 135 us -> 166 us (1.23)
  local copies, waits for them, and re-layouts: 6.32 us -> 37.5 us
    unnamed x12 -> x43, local copies, waits for them, and re-layouts: 0.04 us -> 24.7 us
    another operation x2 -> x4, local copies, waits for them, and re-layouts: 0.06 us -> 6.75 us  [the longest x2 6.69 us: body(): jnp.stack(jnp.split(result_rows, lax.axis_size(('wide', 'narrow')), axis=0))]
where the time goes in v1:
time: 166 us
  blocking collectives  103 us (62%)
  local copies, waits for them, and re-layouts  37.5 us (23%)
  matrix products  13.6 us (8%)
  other arithmetic  6 us (4%)
  starting transfers between devices  5.33 us (3%)
    unnamed x43, local copies, waits for them, and re-layouts  24.7 us
    all_gather x1, blocking collectives, body(): lax.all_gather(sample_out, 'narrow', axis=0, tiled=True)  16.4 us
    all_gather x1, blocking collectives, body(): lax.all_gather(feature_out, 'narrow', axis=0, tiled=True)  15.2 us
    all_gather x1, blocking collectives, body(): lax.all_gather(feature_in, 'narrow', axis=0, tiled=True)  14.4 us
    all_gather x1, blocking collectives, body(): lax.all_gather(hidden_down, 'narrow', axis=0, tiled=True)  14.4 us
    all_gather x1, blocking collectives, body(): lax.all_gather(hidden_up, 'narrow', axis=0, tiled=True)  14.3 us
    all_to_all x1, blocking collectives, body(): lax.all_to_all(jnp.stack(jnp.split(result_rows, lax.axis_size(('wide', 'n...  14.2 us
    all_gather x1, blocking collectives, body(): lax.all_gather(sample_in, 'narrow', axis=0, tiled=True)  13.8 us
  transfers between devices with their start and end apart: 1, of which 0 were waited for; matrix products, arithmetic and copies ran while one was open for 0% of the time, Pallas kernels for 0%

profile of v1, /device:TPU:0, one launch (start us, length us, event | category | flops | bytes accessed | tf_op | source)
XLA Modules:
  0.0 165.8 jit_solution(11421872775888402559)
XLA Ops:
  0.8 15.2 %all_gather.19 = bf16[192,192]{1,0:T(8,128)(2,1)S(1)} all-gather(bf16[48,192]{1,0:T(8,128)(2,1)} %param.19), channel_id=1, replica_groups=mesh['groups'=1,'wide'=8,'narrow'=4] {'narrow'}, dimensions={0}, use_global_device_ids=true | all-gather | bytes 92160 | tf_op jit(solution)/shard_map/all_gather | solution.py:62
  16.0 14.4 %all_gather.18 = bf16[192,576]{1,0:T(8,128)(2,1)S(1)} all-gather(bf16[48,576]{1,0:T(8,128)(2,1)} %param.18), channel_id=1, replica_groups=mesh['groups'=1,'wide'=8,'narrow'=4] {'narrow'}, dimensions={0}, use_global_device_ids=true | all-gather | bytes 276480 | tf_op jit(solution)/shard_map/all_gather | solution.py:61
  30.5 1.3 convolution_convert_fusion.3
  31.8 9.3 %while.22 = (s32[]{:T(128)}, bf16[4,128,192]{1,2,0:T(8,128)(2,1)S(1)}, bf16[4,128,576]{1,2,0:T(8,128)(2,1)S(1)}, s32[4]{0:T(128)S(1)}, s32[]{:T(128)}) while((s32[]{:T(128)}, bf16[4,128,192]{1,2,0:T(8,128)(2,1)S(1)}, bf16[4,128,576]{1,2,0:T(8,128)(2,1)S(1)}, s32[4]{0:T(128)S(1)}, s32[]{:T(128)}) %tuple.61), condition=%wide.region_3.4_spmd.clone, body=%wide.region_0.3_spmd.clone.sunk | while | flops 19981440 | bytes 1776221 | solution.py:70
  41.6 0.9 copy.108
  42.5 5.3 %all-to-all-start = ((bf16[4,128,192]{2,0,1:T(4,128)(2,1)}), bf16[4,128,192]{2,0,1:T(4,128)(2,1)S(1)}, u32[]{:S(2)}, u32[]{:S(2)}) async-start(bf16[4,128,192]{2,0,1:T(4,128)(2,1)} %copy.108), calls=%async_computation | async-start | bytes 524288 | tf_op jit(solution)/shard_map/all_to_all | solution.py:73
  47.8 16.4 %all_gather.21 = bf16[192,192]{1,0:T(8,128)(2,1)S(1)} all-gather(bf16[48,192]{1,0:T(8,128)(2,1)S(1)} %copy-done.4), channel_id=1, replica_groups=mesh['groups'=1,'wide'=8,'narrow'=4] {'narrow'}, dimensions={0}, use_global_device_ids=true | all-gather | bytes 92160 | tf_op jit(solution)/shard_map/all_gather | solution.py:77
  64.3 13.8 %all_gather.20 = bf16[192,576]{1,0:T(8,128)(2,1)S(1)} all-gather(bf16[48,576]{1,0:T(8,128)(2,1)S(1)} %copy-done.3), channel_id=1, replica_groups=mesh['groups'=1,'wide'=8,'narrow'=4] {'narrow'}, dimensions={0}, use_global_device_ids=true | all-gather | bytes 276480 | tf_op jit(solution)/shard_map/all_gather | solution.py:76
  78.0 14.3 %all_gather.22 = bf16[192,768]{1,0:T(8,128)(2,1)S(1)} all-gather(bf16[48,768]{1,0:T(8,128)(2,1)S(1)} %copy-done.2), channel_id=1, replica_groups=mesh['groups'=1,'wide'=8,'narrow'=4] {'narrow'}, dimensions={0}, use_global_device_ids=true | all-gather | bytes 368640 | tf_op jit(solution)/shard_map/all_gather | solution.py:88
  92.3 14.4 %all_gather.23 = bf16[768,192]{1,0:T(8,128)(2,1)S(1)} all-gather(bf16[192,192]{1,0:T(8,128)(2,1)S(1)} %copy-done.1), channel_id=1, replica_groups=mesh['groups'=1,'wide'=8,'narrow'=4] {'narrow'}, dimensions={0}, use_global_device_ids=true | all-gather | bytes 368640 | tf_op jit(solution)/shard_map/all_gather | solution.py:89
  107.4 6.4 %while.23 = (s32[]{:T(128)}, bf16[4,128,192]{1,2,0:T(8,128)(2,1)S(1)}, bf16[4,128,576]{1,2,0:T(8,128)(2,1)S(1)}, s32[]{:T(128)}, s32[]{:T(128)}) while((s32[]{:T(128)}, bf16[4,128,192]{1,2,0:T(8,128)(2,1)S(1)}, bf16[4,128,576]{1,2,0:T(8,128)(2,1)S(1)}, s32[]{:T(128)}, s32[]{:T(128)}) %tuple.58), condition=%wide.region_9.10_spmd.clone, body=%wide.region_6.9_spmd.clone.sunk | while | flops 19981440 | bytes 1776209 | solution.py:82
  115.2 3.8 %fusion.46 = (f32[4,128]{1,0:T(4,128)S(1)}, f32[4,128,192]{1,2,0:T(8,128)S(1)}) fusion(bf16[4,128,192]{1,2,0:T(8,128)(2,1)S(1)} %multiply_convert_fusion, bf16[768,192]{1,0:T(8,128)(2,1)S(1)} %all_gather.23, f32[4,128,768]{2,1,0:T(8,128)S(1)} %get-tuple-element.114, u8[128,768]{1,0:T(8,128)(4,1)S(1)} %get-tuple-element.78, ...), kind=kOutput, calls=%fused_computation.80 | convolution fusion | flops 178814464 | bytes 2656256 | tf_op jit(solution)/shard_map/dot_general | solution.py:42
  124.7 0.8 fusion.75
  127.9 0.8 fusion.71
  131.0 0.8 fusion.67
  131.9 0.8 fusion.66
  139.0 0.8 fusion.57
  139.8 0.8 fusion.56
  141.4 0.8 fusion.54
  143.0 0.8 fusion.52
  143.9 0.8 fusion.51
  144.7 5.9 %copy.113 = bf16[32,4,4,192]{3,2,1,0:T(4,128)(2,1)S(1)} copy(bf16[32,4,4,192]{1,3,2,0:T(8,128)(2,1)} %fusion.51) | data formatting | bytes 393216 | tf_op jit(solution)/shard_map/stack | solution.py:97
  150.6 14.2 %all_to_all.23 = bf16[32,4,4,192]{3,2,1,0:T(4,128)(2,1)S(1)} all-to-all(bf16[32,4,4,192]{3,2,1,0:T(4,128)(2,1)S(1)} %copy.113), channel_id=1, replica_groups=mesh['groups'=1,'wide'=8,'narrow'=4] {'wide','narrow'}, dimensions={0} | all-to-all | bytes 393216 | tf_op jit(solution)/shard_map/all_to_all | solution.py:96
  164.9 0.9 copy.115
  (118 shorter events, 37.1 us)
Async XLA Ops:
  0.0 31.8 %copy-start.5 = (s32[4]{0:T(128)S(1)}, s32[4]{0:T(128)}, u32[]{:S(2)}) copy-start(s32[4]{0:T(128)} %param.15) | copy-start | bytes 52
  31.8 9.3 %copy-start = (bf16[4,128,192]{1,2,0:T(8,128)(2,1)S(1)}, bf16[4,128,192]{1,2,0:T(8,128)(2,1)}, u32[]{:S(2)}) copy-start(bf16[4,128,192]{1,2,0:T(8,128)(2,1)} %param.14) | copy-start | bytes 589828
  41.1 6.7 %copy-start.4 = (bf16[48,192]{1,0:T(8,128)(2,1)S(1)}, bf16[48,192]{1,0:T(8,128)(2,1)}, u32[]{:S(2)}) copy-start(bf16[48,192]{1,0:T(8,128)(2,1)} %param.21) | copy-start | bytes 55300
  41.1 23.2 %copy-start.3 = (bf16[48,576]{1,0:T(8,128)(2,1)S(1)}, bf16[48,576]{1,0:T(8,128)(2,1)}, u32[]{:S(2)}) copy-start(bf16[48,576]{1,0:T(8,128)(2,1)} %param.20) | copy-start | bytes 165892
  41.1 36.9 %copy-start.2 = (bf16[48,768]{1,0:T(8,128)(2,1)S(1)}, bf16[48,768]{1,0:T(8,128)(2,1)}, u32[]{:S(2)}) copy-start(bf16[48,768]{1,0:T(8,128)(2,1)} %param.22) | copy-start | bytes 221188
  41.4 50.9 %copy-start.1 = (bf16[192,192]{1,0:T(8,128)(2,1)S(1)}, bf16[192,192]{1,0:T(8,128)(2,1)}, u32[]{:S(2)}) copy-start(bf16[192,192]{1,0:T(8,128)(2,1)} %param.23) | copy-start | bytes 221188
  42.5 64.2 %all-to-all-start = ((bf16[4,128,192]{2,0,1:T(4,128)(2,1)}), bf16[4,128,192]{2,0,1:T(4,128)(2,1)S(1)}, u32[]{:S(2)}, u32[]{:S(2)}) async-start(bf16[4,128,192]{2,0,1:T(4,128)(2,1)} %copy.108), calls=%async_computation | async-start | bytes 524288 | tf_op jit(solution)/shard_map/all_to_all | solution.py:73
